TPU v7x, 32 devices: a whole 2x2x4 slice. The times are simulated.
32 devices in a mesh: seq: 8 (over y, x, core), head: 4 (over z).
Axes of the slice: x: 2, y: 2, z: 4, core: 2. Of those that a mesh axis runs over, the one named last changes fastest.
Arguments:
- inputs: bfloat16 [2048, 4096], P('seq'), may hold values from -6 to 6
- x_weight: bfloat16 [4096, 8192], P('seq', 'head'), may hold values from -0.125 to 0.125
- b_values: bfloat16 [2048, 8, 128], P('seq'), may hold values from -0.5 to 0.5
- c_values: bfloat16 [2048, 8, 128], P('seq'), may hold values from -0.375 to 0.375
- gate_z: bfloat16 [2048, 8192], P('seq', 'head'), may hold values from -6 to 6
- log_decay: float32 [2048, 128], P('seq', 'head'), may hold values from -2 to 0
- skip_gain: float32 [128], P('head'), may hold values from 0.5 to 1.5
- grad_out: bfloat16 [2048, 8192], P('seq', 'head'), may hold values from -6 to 6
Outputs:
- input_grad: bfloat16 [2048, 4096], P('seq', 'head')
- z_grad: bfloat16 [2048, 8192], P('seq', 'head')
All inputs are finite; a program needn't handle non-finite values.
Results may differ from a plain program's by a relative error of at most 0.0095.
Values may be sent and summed in bfloat16 or wider, within the bound.
A program may use at most 128 MiB of HBM per device.

v0:
```python
import jax
import jax.numpy as jnp
from jax import lax
from jax.sharding import PartitionSpec as P

HEADS = 128
HEAD_DIM = 64
STATE = 128
GROUPS = 8
SPAN = 256
EXACT_MODE = lax.Precision.HIGHEST


def prefix_2(array, axis, combine, identity):
    size, place = (lax.axis_size(axis), lax.axis_index(axis))
    everything = jax.tree.map(
        lambda part, kind: lax.all_gather(part.astype(kind), axis),
        array,
        (jnp.bfloat16, jnp.bfloat16),
    )
    start = jax.tree.map(
        lambda part, zero: jnp.broadcast_to(jnp.asarray(zero, part.dtype), part.shape),
        array,
        identity,
    )

    def prefix_hop(k, before):
        reached = k < place
        new = combine(
            before, jax.tree.map(lambda part, own: part[k].astype(own.dtype), everything, array)
        )
        return jax.tree.map(lambda a, b: jnp.where(reached, a, b), new, before)

    return lax.fori_loop(0, size, prefix_hop, start)


def entering(value, axis, join, neutral):
    count, mine = (lax.axis_size(axis), lax.axis_index(axis))
    pieces = jax.tree.map(lambda part: lax.all_gather(part, axis), value)
    pieces = jax.tree.map(lambda part: part[::-1], pieces)
    mine = count - 1 - mine
    so_far = jax.tree.map(
        lambda part, zero: jnp.full_like(part, 0) + jnp.asarray(zero, part.dtype), value, neutral
    )

    def entering_hop(position, so_far):
        longer = join(so_far, jax.tree.map(lambda part: part[position], pieces))
        return jax.tree.map(lambda new, old: jnp.where(position < mine, new, old), longer, so_far)

    return lax.fori_loop(0, count - 1, entering_hop, so_far)


def decayed_scores(c_block, b_block, prefix):
    scores = jnp.einsum("thn,shn->hts", c_block, b_block, preferred_element_type=jnp.float32)
    later = prefix.T[:, :, None]
    earlier = prefix.T[:, None, :]
    positions = jnp.arange(prefix.shape[0])
    causal = (positions[:, None] >= positions[None, :])[None, :, :]
    spacing = jnp.where(causal, later - earlier, 0.0)
    factors = jnp.where(causal, jnp.exp(spacing), 0.0)
    return (scores * factors).astype(jnp.bfloat16)


def compose(earlier, later):
    return (earlier[0] * later[0], later[0][:, None, None] * earlier[1] + later[1])


def body(inputs, x_weight, b_values, c_values, gate_z, log_decay, skip_gain, grad_out):
    token_count = inputs.shape[0]
    head_count = log_decay.shape[1]
    width_here = x_weight.shape[1]
    block_count = token_count // SPAN
    full_weight = lax.all_gather(x_weight, "seq", axis=0, tiled=True)
    x_sums = jnp.dot(inputs, full_weight, preferred_element_type=jnp.float32)
    x_values = x_sums.astype(jnp.bfloat16)
    first_head = lax.axis_index("head") * head_count
    owners = (first_head + jnp.arange(head_count)) // (HEADS // GROUPS)
    picker = (owners[:, None] == jnp.arange(GROUPS)[None, :]).astype(jnp.bfloat16)
    b_heads = jnp.einsum(
        "tgn,hg->thn", b_values, picker, preferred_element_type=jnp.float32
    ).astype(jnp.bfloat16)
    c_heads = jnp.einsum(
        "tgn,hg->thn", c_values, picker, preferred_element_type=jnp.float32
    ).astype(jnp.bfloat16)
    x_blocks = x_values.reshape(block_count, SPAN, head_count, HEAD_DIM)
    b_blocks = b_heads.reshape(block_count, SPAN, head_count, STATE)
    c_blocks = c_heads.reshape(block_count, SPAN, head_count, STATE)
    prefix = jnp.cumsum(log_decay.reshape(block_count, SPAN, head_count), axis=1)
    totals = prefix[:, -1, :]
    gate = gate_z.astype(jnp.float32).reshape(token_count, head_count, HEAD_DIM)
    upstream = grad_out.astype(jnp.float32).reshape(token_count, head_count, HEAD_DIM)
    sigma = jax.nn.sigmoid(gate)
    y_grad = upstream * gate * sigma
    grad_blocks = y_grad.reshape(block_count, SPAN, head_count, HEAD_DIM)
    low_blocks = grad_blocks.astype(jnp.bfloat16)
    tails = jnp.exp(totals[:, None, :] - prefix)
    fresh_states = jnp.einsum(
        "kshp,kshn->khpn",
        x_blocks.astype(jnp.float32) * tails[..., None],
        b_blocks.astype(jnp.float32),
        precision=EXACT_MODE,
    )
    fresh_grads = jnp.einsum(
        "kthp,kthn->khpn",
        grad_blocks * jnp.exp(prefix)[..., None],
        c_blocks.astype(jnp.float32),
        precision=EXACT_MODE,
    )
    running = jnp.cumsum(totals, axis=0)
    after = running[-1][None, :] - running
    before = running - totals
    device_decay = jnp.exp(running[-1])
    device_state = jnp.einsum("kh,khpn->hpn", jnp.exp(after), fresh_states, precision=EXACT_MODE)
    device_grad = jnp.einsum("kh,khpn->hpn", jnp.exp(before), fresh_grads, precision=EXACT_MODE)
    unit_decay = jnp.ones((head_count,), jnp.float32)
    start_state = prefix_2(
        (device_decay, device_state), "seq", compose, (unit_decay, jnp.zeros_like(device_state))
    )[1]
    end_grad = entering(
        (device_decay, device_grad), "seq", compose, (unit_decay, jnp.zeros_like(device_grad))
    )[1]
    gain = skip_gain[None, :, None]

    def forward(state, items):
        x_block, b_block, c_block, prefix_block, fresh = items
        weights = decayed_scores(c_block, b_block, prefix_block)
        local = jnp.einsum("hts,shp->thp", weights, x_block, preferred_element_type=jnp.float32)
        carried = jnp.exp(prefix_block)[:, :, None] * jnp.einsum(
            "thn,hpn->thp", c_block.astype(jnp.float32), state, precision=EXACT_MODE
        )
        state = jnp.exp(prefix_block[-1])[:, None, None] * state + fresh
        return (state, (local + carried + gain * x_block.astype(jnp.float32), weights))

    final_state, (outputs, weight_blocks) = lax.scan(
        forward, start_state, (x_blocks, b_blocks, c_blocks, prefix, fresh_states)
    )
    outputs = outputs.reshape(token_count, head_count, HEAD_DIM)
    z_grad = (upstream * outputs * sigma * (1.0 + gate * (1.0 - sigma))).astype(jnp.bfloat16)
    z_grad = z_grad.reshape(token_count, width_here)

    def backward(carry, items):
        weights, b_block, tail_block, total_block, grad_block, low_block, fresh = items
        local = jnp.einsum("hts,thp->shp", weights, low_block, preferred_element_type=jnp.float32)
        carried = tail_block[:, :, None] * jnp.einsum(
            "shn,hpn->shp", b_block.astype(jnp.float32), carry, precision=EXACT_MODE
        )
        carry = jnp.exp(total_block)[:, None, None] * carry + fresh
        return (carry, local + carried + gain * grad_block)

    final_grad, x_grads = lax.scan(
        backward,
        end_grad,
        (weight_blocks, b_blocks, tails, totals, grad_blocks, low_blocks, fresh_grads),
        reverse=True,
    )
    x_grad = x_grads.reshape(token_count, width_here).astype(jnp.bfloat16)
    partial_sums = jnp.einsum("tk,dk->td", x_grad, full_weight, preferred_element_type=jnp.float32)
    input_grad = lax.psum_scatter(
        partial_sums.astype(jnp.bfloat16), "head", scatter_dimension=1, tiled=True
    )
    return (input_grad, z_grad)


def solution(mesh):
    in_specs = (
        P("seq", None),
        P("seq", "head"),
        P("seq", None, None),
        P("seq", None, None),
        P("seq", "head"),
        P("seq", "head"),
        P("head"),
        P("seq", "head"),
    )
    out_specs = (P("seq", "head"), P("seq", "head"))
    return jax.shard_map(body, mesh=mesh, in_specs=in_specs, out_specs=out_specs, check_vma=False)
```

profile of v0, /device:TPU:0, one launch (start us, length us, event | category | flops | bytes accessed | tf_op | source)
XLA Modules:
  0.0 324.2 jit_solution(4623977196892682287)
XLA Ops:
  7.2 0.7 all-gather.8.cloned.1.call-update
  8.0 0.1 copy-done.10
  8.1 0.6 reduce-window.6
  8.7 0.2 slice_reduce_fusion
  8.9 0.1 copy.72
  9.1 0.7 copy.75
  9.8 2.0 convert_bitcast_fusion
  11.9 90.6 %all-gather.8.cloned.1.call-done = bf16[4096,2048]{1,0:T(8,128)(2,1)} async-done(((bf16[512,2048]{1,0:T(8,128)(2,1)}), bf16[4096,2048]{1,0:T(8,128)(2,1)}) %all-gather.8.cloned.1.call-update) | async-done | bytes 16777232 | tf_op jit(solution)/shard_map/all_gather | solution.py:73
  102.5 8.3 %convolution_convert_fusion.1 = bf16[256,2048]{1,0:T(8,128)(2,1)S(1)} fusion(bf16[256,4096]{1,0:T(8,128)(2,1)S(1)} %copy-done, bf16[4096,2048]{1,0:T(8,128)(2,1)} %all-gather.8.cloned.1.call-done), kind=kOutput, calls=%fused_computation.14 | convolution fusion | flops 4295491584 | bytes 19922944 | tf_op jit(solution)/shard_map/dot_general | solution.py:74
  110.8 0.5 copy.79
  111.3 0.2 copy-done.8
  111.5 4.3 %fusion.32 = bf16[32,64,128]{2,1,0:T(8,128)(2,1)} fusion(bf16[256,32,128]{2,1,0:T(8,128)(2,1)} %convert_bitcast_fusion, bf16[256,32,64]{0,2,1:T(8,128)(2,1)S(1)} %bitcast.101, f32[256,32]{0,1:T(8,128)S(1)} %copy-done.8, f32[32]{0:T(128)S(1)} %subtract_exponential_fusion), kind=kOutput, calls=%fused_computation.43 | convolution fusion | flops 806879232 | bytes 3702912 | tf_op jit(solution)/shard_map/kshp,kshn->khpn/dot_general | solution.py:97
  116.0 8.9 %all-gather.3 = bf16[8,1,32]{2,1,0:T(2,128)(2,1)S(1)} all-gather(bf16[1,1,32]{2,1,0:T(2,128)(2,1)S(1)} %get-tuple-element.325), channel_id=5, replica_groups=mesh['seq'=8,'head'=4] {'seq'}, dimensions={0}, use_global_device_ids=true | all-gather | bytes 576 | tf_op jit(solution)/shard_map/all_gather | solution.py:17
  125.1 0.7 convert_bitcast_fusion.1
  125.8 0.8 copy-done.4
  126.6 6.0 %multiply_convert_fusion = bf16[32,256,256]{2,1,0:T(8,128)(2,1)S(1)} fusion(f32[32,256]{1,0:T(8,128)S(1)} %copy.73, pred[256,256]{1,0:T(8,128)(4,1)S(1)} %iota_compare_fusion, bf16[256,32,128]{2,1,0:T(8,128)(2,1)S(1)} %copy-done.4, bf16[256,32,128]{2,1,0:T(8,128)(2,1)S(1)} %convert_bitcast_fusion.1), kind=kOutput, calls=%fused_computation.6 | convolution fusion | flops 547356672 | bytes 8486912 | tf_op jit(solution)/shard_map/while/body/eval_jaxpr/thn,shn->hts/dot_general | solution.py:54
  132.7 2.0 copy-done.3
  134.6 2.7 fusion.45
  137.4 15.4 %all-gather.12.cloned.1.call-done = bf16[256,64,128]{2,1,0:T(8,128)(2,1)} async-done(((bf16[32,64,128]{2,1,0:T(8,128)(2,1)}), bf16[256,64,128]{2,1,0:T(8,128)(2,1)}) %all-gather.12.cloned.1.call-update) | async-done | bytes 4194320 | tf_op jit(solution)/shard_map/all_gather | solution.py:17
  152.8 10.7 %while.19 = (s32[]{:T(128)}, f32[32,64,128]{2,1,0:T(8,128)S(1)}, s32[]{:T(128)}, bf16[8,32]{1,0:T(8,128)(2,1)S(1)}, bf16[8,32,64,128]{3,2,1,0:T(8,128)(2,1)}, /*index=5*/s32[]{:T(128)}, s32[]{:T(128)}) while((s32[]{:T(128)}, f32[32,64,128]{2,1,0:T(8,128)S(1)}, s32[]{:T(128)}, bf16[8,32]{1,0:T(8,128)(2,1)S(1)}, ...), condition=%wide.region_6.7_spmd.clone, body=%wide.region_5.6_spmd.clone.sunk | while | flops 1310756 | bytes 2621873 | solution.py:34
  152.8 1.3 fusion.61
  154.1 1.3 fusion.61
  155.4 1.3 fusion.61
  156.8 1.3 fusion.61
  158.1 1.3 fusion.61
  159.5 1.3 fusion.61
  160.8 1.3 fusion.61
  162.1 1.3 fusion.61
  163.5 6.3 %fusion.6 = f32[256,32,64]{0,2,1:T(8,128)} fusion(bf16[256,32,64]{0,2,1:T(8,128)(2,1)S(1)} %bitcast.103, f32[32,64,256]{2,1,0:T(8,128)} %fusion.45, f32[32,64,128]{2,1,0:T(8,128)S(1)} %get-tuple-element.254, bf16[256,32,128]{2,1,0:T(8,128)(2,1)} %copy-done.2, f32[256,32]{0,1:T(8,128)S(1)} %copy.80, f32[32]{0:T(128)S(1)} %copy-done.11), kind=kOutput, calls=%fused_computation.19 | convolution fusion | flops 807927808 | bytes 8421504 | tf_op jit(solution)/shard_map/while/body/eval_jaxpr/thn,hpn->thp/dot_general | solution.py:128
  169.8 2.0 copy.83
  171.8 3.9 %fusion.4 = (bf16[256,2048]{1,0:T(8,128)(2,1)}, f32[256,2048]{1,0:T(8,128)}) fusion(f32[256,2048]{1,0:T(8,128)S(1)} %copy.83, bf16[256,2048]{1,0:T(8,128)(2,1)S(1)} %copy-done.5, bf16[256,2048]{1,0:T(8,128)(2,1)} %param.16), kind=kLoop, calls=%fused_computation.17 | loop fusion | flops 7340032 | bytes 7340032 | tf_op jit(solution)/shard_map/convert_element_type | solution.py:138
  175.7 1.9 copy.67
  177.6 4.5 %fusion.24 = f32[32,64,128]{2,1,0:T(8,128)} fusion(bf16[256,32,128]{2,1,0:T(8,128)(2,1)} %copy-done.2, f32[256,32,64]{0,2,1:T(8,128)S(1)} %bitcast.98, f32[256,32]{0,1:T(8,128)S(1)} %copy.76, f32[32]{0:T(128)S(1)} %subtract_exponential_fusion), kind=kOutput, calls=%fused_computation.41 | convolution fusion | flops 806092800 | bytes 5275776 | tf_op jit(solution)/shard_map/kthp,kthn->khpn/dot_general | solution.py:103
  182.3 8.9 %all-gather = f32[8,1,32]{2,1,0:T(1,128)S(1)} all-gather(f32[1,1,32]{2,1,0:T(1,128)S(1)} %get-tuple-element.327), channel_id=2, replica_groups=mesh['seq'=8,'head'=4] {'seq'}, dimensions={0}, use_global_device_ids=true | all-gather | bytes 1152 | tf_op jit(solution)/shard_map/all_gather | solution.py:39
  191.2 4.5 %fusion.37 = f32[32,64,256]{2,1,0:T(8,128)} fusion(bf16[32,256,256]{2,1,0:T(8,128)(2,1)} %copy-done.3, f32[256,32,64]{0,2,1:T(8,128)S(1)} %bitcast.99), kind=kOutput, calls=%fused_computation.46 | convolution fusion | flops 268959744 | bytes 8388608 | tf_op jit(solution)/shard_map/while/body/eval_jaxpr/hts,thp->shp/dot_general | solution.py:143
  195.7 41.1 %all-gather.10.cloned.1.call-done = f32[256,64,128]{2,1,0:T(8,128)} async-done(((f32[32,64,128]{2,1,0:T(8,128)}), f32[256,64,128]{2,1,0:T(8,128)}) %all-gather.10.cloned.1.call-update) | async-done | bytes 8388624 | tf_op jit(solution)/shard_map/all_gather | solution.py:39
  236.7 8.3 %rev.7 = f32[8,32,64,128]{3,2,1,0:T(8,128)} reverse(f32[8,32,64,128]{3,2,1,0:T(8,128)} %bitcast.104), dimensions={0} | reverse | bytes 16777216 | tf_op jit(solution)/shard_map/rev | solution.py:40
  245.0 10.5 %while.18 = (s32[]{:T(128)}, f32[32,64,128]{2,1,0:T(8,128)S(1)}, s32[]{:T(128)}, f32[8,32]{1,0:T(8,128)S(1)}, f32[8,32,64,128]{3,2,1,0:T(8,128)}, /*index=5*/s32[]{:T(128)}, s32[]{:T(128)}) while((s32[]{:T(128)}, f32[32,64,128]{2,1,0:T(8,128)S(1)}, s32[]{:T(128)}, f32[8,32]{1,0:T(8,128)S(1)}, f32[8,32,64,128]{3,2,1,0:T(8,128)}, ...), condition=%wide.region_3.4_spmd.clone, body=%wide.region_2.3_spmd.clone.sunk | while | flops 1048580 | bytes 3146225 | solution.py:50
  245.0 1.5 fusion.60
  246.5 1.5 fusion.60
  248.0 1.5 fusion.60
  249.6 1.5 fusion.60
  251.1 1.5 fusion.60
  252.6 1.5 fusion.60
  254.1 1.5 fusion.60
  255.6 5.9 %fusion.15 = bf16[256,32,64]{0,2,1:T(8,128)(2,1)} fusion(f32[32,64,256]{2,1,0:T(8,128)} %fusion.37, f32[256,32,64]{0,2,1:T(8,128)S(1)} %bitcast.100, f32[32,64,128]{2,1,0:T(8,128)S(1)} %get-tuple-element.253, bf16[256,32,128]{2,1,0:T(8,128)(2,1)} %convert_bitcast_fusion, f32[32]{0:T(128)S(1)} %copy-done.11, f32[256,32]{0,1:T(8,128)S(1)} %copy-done.9), kind=kOutput, calls=%fused_computation.30 | convolution fusion | flops 807927808 | bytes 8421504 | tf_op jit(solution)/shard_map/while/body/eval_jaxpr/shn,hpn->shp/dot_general | solution.py:144
  261.5 12.1 %convolution_convert_fusion = bf16[256,4096]{1,0:T(8,128)(2,1)} fusion(bf16[256,2048]{0,1:T(8,128)(2,1)} %bitcast.110, bf16[4096,2048]{1,0:T(8,128)(2,1)} %all-gather.8.cloned.1.call-done), kind=kOutput, calls=%fused_computation.7 | convolution fusion | flops 4296015872 | bytes 19922944 | tf_op jit(solution)/shard_map/tk,dk->td/dot_general | solution.py:157
  273.6 44.0 %reduce-scatter.2.cloned.1.call-done = bf16[256,1024]{1,0:T(8,128)(2,1)} async-done(((bf16[256,4096]{1,0:T(8,128)(2,1)}), bf16[256,1024]{1,0:T(8,128)(2,1)}) %reduce-scatter.2.cloned.1.call-update) | async-done | bytes 524304 | tf_op jit(solution)/shard_map/reduce_scatter | solution.py:158
  (59 shorter events, 0.8 us)
Async XLA Ops:
  7.2 95.4 %copy-start = (bf16[256,4096]{1,0:T(8,128)(2,1)S(1)}, bf16[256,4096]{1,0:T(8,128)(2,1)}, u32[]{:S(2)}) copy-start(bf16[256,4096]{1,0:T(8,128)(2,1)} %param.12) | copy-start | bytes 6291460
  7.2 0.9 copy-start.10
  7.2 2.6 copy-start.6
  7.2 95.3 %all-gather.8.cloned.1.call-start = ((), (), s32[]{:S(2)}) async-start(), calls=%async_computation.1 | async-start | bytes 18874368 | tf_op jit(solution)/shard_map/all_gather | solution.py:73
  7.9 144.8 %all-gather.12.cloned.1.call-start = ((), (), s32[]{:S(2)}) async-start(), calls=%async_computation.4 | async-start | bytes 4718592 | tf_op jit(solution)/shard_map/all_gather | solution.py:17
  110.8 0.8 copy-start.8
  111.5 13.5 %copy-start.7 = (bf16[256,8,128]{2,1,0:T(8,128)(2,1)S(1)}, bf16[256,8,128]{2,1,0:T(8,128)(2,1)}, u32[]{:S(2)}) copy-start(bf16[256,8,128]{2,1,0:T(8,128)(2,1)} %param.15) | copy-start | bytes 1572868
  115.9 120.9 %all-gather.10.cloned.1.call-start = ((), (), s32[]{:S(2)}) async-start(), calls=%async_computation.3 | async-start | bytes 9437184 | tf_op jit(solution)/shard_map/all_gather | solution.py:39
  125.0 1.6 copy-start.4
  126.6 6.0 %copy-start.2 = (bf16[256,32,128]{2,1,0:T(8,128)(2,1)}, bf16[256,32,128]{2,1,0:T(8,128)(2,1)S(1)}, u32[]{:S(2)}) copy-start(bf16[256,32,128]{2,1,0:T(8,128)(2,1)S(1)} %convert_bitcast_fusion.1) | copy-start | bytes 6291460
  132.6 2.0 copy-start.3
  152.8 10.7 %copy-start.11 = (f32[32]{0:T(128)S(1)}, f32[32]{0:T(128)}, u32[]{:S(2)}) copy-start(f32[32]{0:T(128)} %param.18) | copy-start | bytes 388
  169.8 2.0 copy-start.5
  182.2 135.5 %reduce-scatter.2.cloned.1.call-start = ((), (), s32[]{:S(2)}) async-start(), calls=%async_computation.2 | async-start | bytes 2621440 | tf_op jit(solution)/shard_map/reduce_scatter | solution.py:158
  245.0 10.5 %copy-start.9 = (f32[256,32]{0,1:T(8,128)S(1)}, f32[256,32]{0,1:T(8,128)}, u32[]{:S(2)}) copy-start(f32[256,32]{0,1:T(8,128)} %copy.75) | copy-start | bytes 98308
  261.5 56.2 %copy-start.1 = (bf16[256,4096]{1,0:T(8,128)(2,1)S(1)}, bf16[256,4096]{1,0:T(8,128)(2,1)}, u32[]{:S(2)}) copy-start(bf16[256,4096]{1,0:T(8,128)(2,1)} %param.12) | copy-start | bytes 6291460
Sparse Core Ops, SparseCore 0:
  9.9 92.5 all-gather.7
  116.0 36.7 all-gather.11
  182.3 54.3 all-gather.9
  273.8 43.8 reduce-scatter.1
where the time goes:
time: 325 us; the launch traced here: 324 us
  waiting for transfers between devices  192 us (59%)
  matrix products  57.5 us (18%)
  other arithmetic  25.4 us (8%)
  blocking collectives  17.8 us (5%)
  local copies, waits for them, and re-layouts  17.1 us (5%)
  between operations  14 us (4%)
    all_gather x1, waiting for transfers between devices, body(): full_weight = lax.all_gather(x_weight, 'seq', axis=0, tiled=True)  90.6 us
    reduce_scatter x1, waiting for transfers between devices, body(): lax.psum_scatter(partial_sums.astype(jnp.bfloat16), 'head', scatter_dimen...  44 us
    all_gather x1, waiting for transfers between devices, entering(): pieces = jax.tree.map(lambda part: lax.all_gather(part, axis), value)  41.1 us
    all_gather x1, waiting for transfers between devices, prefix_2(): lax.all_gather(part.astype(kind), axis)  15.4 us
    dot_general x1, matrix products, body(): jnp.einsum('tk,dk->td', x_grad, full_weight, preferred_element_type=jnp.f...  12.1 us
    select_n x8, other arithmetic, prefix_hop(): return jax.tree.map(lambda a, b: jnp.where(reached, a, b), new, before)  10.4 us
    select_n x7, other arithmetic, entering_hop(): jnp.where(position < mine, new, old)  10.3 us
    all_gather x1, blocking collectives, entering(): pieces = jax.tree.map(lambda part: lax.all_gather(part, axis), value)  8.92 us
  transfers between devices with their start and end apart: 4, of which 4 were waited for; matrix products, arithmetic and copies ran while one was open for 6% of the time, Pallas kernels for 0%

commit v1 on v0

--- a/solution.py
+++ b/solution.py
@@ -9,6 +9,17 @@
 GROUPS = 8
 SPAN = 256
 EXACT_MODE = lax.Precision.HIGHEST
+
+
+def gather_by_hops(x, axis, along):
+    size = lax.axis_size(axis)
+    right = [(i, (i + 1) % size) for i in range(size)]
+    shards = [x]
+    for stride in range(1, size):
+        shards = [lax.ppermute(shards[0], axis, right), *shards]
+    out = jnp.concatenate(shards, axis=along)
+    shift = (lax.axis_index(axis) + 1) * shards[-1].shape[along]
+    return jnp.roll(out, shift, axis=along)
 
 
 def prefix_2(array, axis, combine, identity):
@@ -70,7 +81,7 @@
     head_count = log_decay.shape[1]
     width_here = x_weight.shape[1]
     block_count = token_count // SPAN
-    full_weight = lax.all_gather(x_weight, "seq", axis=0, tiled=True)
+    full_weight = gather_by_hops(x_weight, "seq", 0)
     x_sums = jnp.dot(inputs, full_weight, preferred_element_type=jnp.float32)
     x_values = x_sums.astype(jnp.bfloat16)
     first_head = lax.axis_index("head") * head_count

time: 325 us -> 457 us (1.41)
  waiting for transfers between devices: 192 us -> 282 us
  local copies, waits for them, and re-layouts: 17.1 us -> 58.7 us
    ppermute x0 -> x7, waiting for transfers between devices: none -> 181 us  [gather_by_hops(): shards = [lax.ppermute(shards[0], axis, right), *shards]]
    all_gather x1 -> x0, waiting for transfers between devices: 90.6 us -> none  [body(): full_weight = lax.all_gather(x_weight, 'seq', axis=0, tiled=True)]
    unnamed x25 -> x60, local copies, waits for them, and re-layouts: 3.12 us -> 43 us
  transfers between devices with their start and end apart: 4 -> 10, of which waited for: 4 -> 10; matrix products, arithmetic and copies ran while one was open for 6% -> 4% of each run, Pallas kernels for 0% -> 0%
where the time goes in v1:
time: 457 us; the launch traced here: 455 us
  waiting for transfers between devices  282 us (62%)
  local copies, waits for them, and re-layouts  58.7 us (13%)
  matrix products  55.8 us (12%)
  other arithmetic  25.3 us (6%)
  blocking collectives  18.6 us (4%)
  between operations  14 us (3%)
    ppermute x7, waiting for transfers between devices, gather_by_hops(): shards = [lax.ppermute(shards[0], axis, right), *shards]  181 us
    reduce_scatter x1, waiting for transfers between devices, body(): lax.psum_scatter(partial_sums.astype(jnp.bfloat16), 'head', scatter_dimen...  44 us
    unnamed x60, local copies, waits for them, and re-layouts  43 us
    all_gather x1, waiting for transfers between devices, entering(): pieces = jax.tree.map(lambda part: lax.all_gather(part, axis), value)  41.1 us
    all_gather x1, waiting for transfers between devices, prefix_2(): lax.all_gather(part.astype(kind), axis)  15.6 us
    dot_general x1, matrix products, body(): jnp.einsum('tk,dk->td', x_grad, full_weight, preferred_element_type=jnp.f...  12.1 us
    select_n x8, other arithmetic, prefix_hop(): return jax.tree.map(lambda a, b: jnp.where(reached, a, b), new, before)  10.4 us
    select_n x7, other arithmetic, entering_hop(): jnp.where(position < mine, new, old)  10.2 us
  transfers between devices with their start and end apart: 10, of which 10 were waited for; matrix products, arithmetic and copies ran while one was open for 4% of the time, Pallas kernels for 0%

profile of v1, /device:TPU:0, one launch (start us, length us, event | category | flops | bytes accessed | tf_op | source)
XLA Modules:
  0.0 455.4 jit_solution(2814309517143871245)
XLA Ops:
  7.7 26.8 %collective-permute-done = bf16[512,2048]{1,0:T(8,128)(2,1)S(1)} collective-permute-done((bf16[512,2048]{1,0:T(8,128)(2,1)}, bf16[512,2048]{1,0:T(8,128)(2,1)S(1)}, u32[]{:S(2)}, u32[]{:S(2)}) %collective-permute-start) | collective-permute-done | bytes 2097184 | tf_op jit(solution)/shard_map/ppermute | solution.py:19
  35.8 26.4 %collective-permute-done.1 = bf16[512,2048]{1,0:T(8,128)(2,1)S(1)} collective-permute-done((bf16[512,2048]{1,0:T(8,128)(2,1)S(1)}, bf16[512,2048]{1,0:T(8,128)(2,1)S(1)}, u32[]{:S(2)}, u32[]{:S(2)}) %collective-permute-start.1) | collective-permute-done | bytes 2097184 | tf_op jit(solution)/shard_map/ppermute | solution.py:19
  63.6 26.4 %collective-permute-done.2 = bf16[512,2048]{1,0:T(8,128)(2,1)S(1)} collective-permute-done((bf16[512,2048]{1,0:T(8,128)(2,1)S(1)}, bf16[512,2048]{1,0:T(8,128)(2,1)S(1)}, u32[]{:S(2)}, u32[]{:S(2)}) %collective-permute-start.2) | collective-permute-done | bytes 2097184 | tf_op jit(solution)/shard_map/ppermute | solution.py:19
  91.3 26.4 %collective-permute-done.3 = bf16[512,2048]{1,0:T(8,128)(2,1)S(1)} collective-permute-done((bf16[512,2048]{1,0:T(8,128)(2,1)S(1)}, bf16[512,2048]{1,0:T(8,128)(2,1)S(1)}, u32[]{:S(2)}, u32[]{:S(2)}) %collective-permute-start.3) | collective-permute-done | bytes 2097184 | tf_op jit(solution)/shard_map/ppermute | solution.py:19
  119.0 26.4 %collective-permute-done.4 = bf16[512,2048]{1,0:T(8,128)(2,1)S(1)} collective-permute-done((bf16[512,2048]{1,0:T(8,128)(2,1)S(1)}, bf16[512,2048]{1,0:T(8,128)(2,1)S(1)}, u32[]{:S(2)}, u32[]{:S(2)}) %collective-permute-start.4) | collective-permute-done | bytes 2097184 | tf_op jit(solution)/shard_map/ppermute | solution.py:19
  146.7 26.5 %collective-permute-done.5 = bf16[512,2048]{1,0:T(8,128)(2,1)} collective-permute-done((bf16[512,2048]{1,0:T(8,128)(2,1)S(1)}, bf16[512,2048]{1,0:T(8,128)(2,1)}, u32[]{:S(2)}, u32[]{:S(2)}) %collective-permute-start.5) | collective-permute-done | bytes 2097184 | tf_op jit(solution)/shard_map/ppermute | solution.py:19
  175.7 1.8 convert_bitcast_fusion
  177.5 22.4 %collective-permute-done.6 = bf16[512,2048]{1,0:T(8,128)(2,1)} collective-permute-done((bf16[512,2048]{1,0:T(8,128)(2,1)}, bf16[512,2048]{1,0:T(8,128)(2,1)}, u32[]{:S(2)}, u32[]{:S(2)}) %collective-permute-start.6) | collective-permute-done | bytes 2097184 | tf_op jit(solution)/shard_map/ppermute | solution.py:19
  199.8 3.2 constant_dynamic-update-slice_fusion.15
  203.0 3.3 constant_dynamic-update-slice_fusion.14
  206.4 1.5 constant_dynamic-update-slice_fusion.13
  208.7 1.5 constant_dynamic-update-slice_fusion.12
  211.1 1.5 constant_dynamic-update-slice_fusion.11
  213.4 1.5 constant_dynamic-update-slice_fusion.10
  219.6 3.2 constant_dynamic-update-slice_fusion.7
  222.7 3.2 constant_dynamic-update-slice_fusion.6
  225.9 1.5 constant_dynamic-update-slice_fusion.5
  227.4 1.5 constant_dynamic-update-slice_fusion.4
  228.9 1.5 constant_dynamic-update-slice_fusion.3
  230.4 1.5 constant_dynamic-update-slice_fusion.2
  234.8 8.5 %fusion.9 = bf16[2048,256]{1,0:T(8,128)(2,1)S(1)} fusion(bf16[256,4096]{1,0:T(8,128)(2,1)S(1)} %copy-done, bf16[8192,2048]{1,0:T(8,128)(2,1)} %constant_dynamic-update-slice_fusion, s32[]{:T(128)S(6)} %select_n.77), kind=kOutput, calls=%fused_computation.18 | convolution fusion | flops 4295491584 | bytes 19922948 | tf_op jit(solution)/shard_map/dot_general | solution.py:85
  243.4 2.7 fusion.42
  246.2 9.7 %all-gather.3 = bf16[8,1,32]{2,1,0:T(2,128)(2,1)S(1)} all-gather(bf16[1,1,32]{2,1,0:T(2,128)(2,1)S(1)} %get-tuple-element.325), channel_id=5, replica_groups=mesh['seq'=8,'head'=4] {'seq'}, dimensions={0}, use_global_device_ids=true | all-gather | bytes 576 | tf_op jit(solution)/shard_map/all_gather | solution.py:28
  257.7 6.0 %multiply_convert_fusion = bf16[32,256,256]{2,1,0:T(8,128)(2,1)S(1)} fusion(f32[32,256]{1,0:T(8,128)S(1)} %copy.69, pred[256,256]{1,0:T(8,128)(4,1)S(1)} %iota_compare_fusion, bf16[256,32,128]{2,1,0:T(8,128)(2,1)S(1)} %copy-done.16, bf16[256,32,128]{2,1,0:T(8,128)(2,1)S(1)} %convert_bitcast_fusion.1), kind=kOutput, calls=%fused_computation.10 | convolution fusion | flops 547356672 | bytes 8486912 | tf_op jit(solution)/shard_map/while/body/eval_jaxpr/thn,shn->hts/dot_general | solution.py:65
  263.7 1.9 copy-done.3
  265.7 2.8 fusion.57
  268.4 15.6 %all-gather.9.cloned.1.call-done = bf16[256,64,128]{2,1,0:T(8,128)(2,1)} async-done(((bf16[32,64,128]{2,1,0:T(8,128)(2,1)}), bf16[256,64,128]{2,1,0:T(8,128)(2,1)}) %all-gather.9.cloned.1.call-update) | async-done | bytes 4194320 | tf_op jit(solution)/shard_map/all_gather | solution.py:28
  284.1 10.7 %while.19 = (s32[]{:T(128)}, f32[32,64,128]{2,1,0:T(8,128)S(1)}, s32[]{:T(128)}, bf16[8,32]{1,0:T(8,128)(2,1)S(1)}, bf16[8,32,64,128]{3,2,1,0:T(8,128)(2,1)}, /*index=5*/s32[]{:T(128)}, s32[]{:T(128)}) while((s32[]{:T(128)}, f32[32,64,128]{2,1,0:T(8,128)S(1)}, s32[]{:T(128)}, bf16[8,32]{1,0:T(8,128)(2,1)S(1)}, ...), condition=%wide.region_6.7_spmd.clone, body=%wide.region_5.6_spmd.clone.sunk | while | flops 1310756 | bytes 2621865 | solution.py:45
  294.7 6.3 %fusion.16 = f32[256,32,64]{0,2,1:T(8,128)} fusion(bf16[256,32,64]{0,2,1:T(8,128)(2,1)S(1)} %bitcast.105, f32[32,64,256]{2,1,0:T(8,128)} %fusion.57, f32[32,64,128]{2,1,0:T(8,128)S(1)} %get-tuple-element.254, bf16[256,32,128]{2,1,0:T(8,128)(2,1)} %copy-done.2, f32[256,32]{0,1:T(8,128)S(1)} %copy.75, f32[32]{0:T(128)S(1)} %copy-done.21), kind=kOutput, calls=%fused_computation.23 | convolution fusion | flops 807927808 | bytes 8421504 | tf_op jit(solution)/shard_map/while/body/eval_jaxpr/thn,hpn->thp/dot_general | solution.py:139
  301.1 2.0 copy.78
  303.1 3.9 fusion.14
  307.0 1.9 copy.63
  308.9 4.5 fusion.34
  313.5 8.9 %all-gather = f32[8,1,32]{2,1,0:T(1,128)S(1)} all-gather(f32[1,1,32]{2,1,0:T(1,128)S(1)} %get-tuple-element.327), channel_id=2, replica_groups=mesh['seq'=8,'head'=4] {'seq'}, dimensions={0}, use_global_device_ids=true | all-gather | bytes 1152 | tf_op jit(solution)/shard_map/all_gather | solution.py:50
  322.4 4.5 fusion.47
  326.9 41.1 %all-gather.7.cloned.1.call-done = f32[256,64,128]{2,1,0:T(8,128)} async-done(((f32[32,64,128]{2,1,0:T(8,128)}), f32[256,64,128]{2,1,0:T(8,128)}) %all-gather.7.cloned.1.call-update) | async-done | bytes 8388624 | tf_op jit(solution)/shard_map/all_gather | solution.py:50
  368.0 8.3 %rev.7 = f32[8,32,64,128]{3,2,1,0:T(8,128)} reverse(f32[8,32,64,128]{3,2,1,0:T(8,128)} %bitcast.101), dimensions={0} | reverse | bytes 16777216 | tf_op jit(solution)/shard_map/rev | solution.py:51
  376.3 10.5 %while.18 = (s32[]{:T(128)}, f32[32,64,128]{2,1,0:T(8,128)S(1)}, s32[]{:T(128)}, f32[8,32]{1,0:T(8,128)S(1)}, f32[8,32,64,128]{3,2,1,0:T(8,128)}, /*index=5*/s32[]{:T(128)}, s32[]{:T(128)}) while((s32[]{:T(128)}, f32[32,64,128]{2,1,0:T(8,128)S(1)}, s32[]{:T(128)}, f32[8,32]{1,0:T(8,128)S(1)}, f32[8,32,64,128]{3,2,1,0:T(8,128)}, ...), condition=%wide.region_3.4_spmd.clone, body=%wide.region_2.3_spmd.clone.sunk | while | flops 1048580 | bytes 3146217 | solution.py:61
  376.3 1.5 fusion.70
  377.8 1.5 fusion.70
  379.3 1.5 fusion.70
  380.8 1.5 fusion.70
  382.3 1.5 fusion.70
  383.8 1.5 fusion.70
  385.3 1.5 fusion.70
  386.8 5.9 %fusion.25 = bf16[256,32,64]{0,2,1:T(8,128)(2,1)} fusion(f32[32,64,256]{2,1,0:T(8,128)} %fusion.47, f32[256,32,64]{0,2,1:T(8,128)S(1)} %bitcast.100, f32[32,64,128]{2,1,0:T(8,128)S(1)} %get-tuple-element.253, bf16[256,32,128]{2,1,0:T(8,128)(2,1)} %copy-done.15, f32[32]{0:T(128)S(1)} %copy-done.21, f32[256,32]{0,1:T(8,128)S(1)} %copy-done.20), kind=kOutput, calls=%fused_computation.34 | convolution fusion | flops 807927808 | bytes 8421504 | tf_op jit(solution)/shard_map/while/body/eval_jaxpr/shn,hpn->shp/dot_general | solution.py:155
  392.7 12.1 %fusion.6 = bf16[256,4096]{1,0:T(8,128)(2,1)} fusion(bf16[256,2048]{0,1:T(8,128)(2,1)} %bitcast.110, bf16[8192,2048]{1,0:T(8,128)(2,1)} %constant_dynamic-update-slice_fusion, s32[]{:T(128)S(6)} %select_n.77), kind=kOutput, calls=%fused_computation.11 | convolution fusion | flops 4296015872 | bytes 19922948 | tf_op jit(solution)/shard_map/tk,dk->td/dot_general | solution.py:168
  404.8 44.0 %reduce-scatter.2.cloned.1.call-done = bf16[256,1024]{1,0:T(8,128)(2,1)} async-done(((bf16[256,4096]{1,0:T(8,128)(2,1)}), bf16[256,1024]{1,0:T(8,128)(2,1)}) %reduce-scatter.2.cloned.1.call-update) | async-done | bytes 524304 | tf_op jit(solution)/shard_map/reduce_scatter | solution.py:169
  (105 shorter events, 32.3 us)
Async XLA Ops:
  7.2 227.7 %copy-start = (bf16[256,4096]{1,0:T(8,128)(2,1)S(1)}, bf16[256,4096]{1,0:T(8,128)(2,1)}, u32[]{:S(2)}) copy-start(bf16[256,4096]{1,0:T(8,128)(2,1)} %param.12) | copy-start | bytes 6291460
  7.2 276.9 %all-gather.9.cloned.1.call-start = ((), (), s32[]{:S(2)}) async-start(), calls=%async_computation.3 | async-start | bytes 4718592 | tf_op jit(solution)/shard_map/all_gather | solution.py:28
  7.2 27.3 %collective-permute-start = (bf16[512,2048]{1,0:T(8,128)(2,1)}, bf16[512,2048]{1,0:T(8,128)(2,1)S(1)}, u32[]{:S(2)}, u32[]{:S(2)}) collective-permute-start(bf16[512,2048]{1,0:T(8,128)(2,1)} %param.13), channel_id=1, source_target_pairs={{0,4},{4,8},{8,12},{12,16},{16,20},{20,24},{24,28},{28,0},{1,5},{5... | collective-permute-start | bytes 6291464 | tf_op jit(solution)/shard_map/ppermute | solution.py:19
  34.5 1.3 copy-start.5
  35.8 26.4 %collective-permute-start.1 = (bf16[512,2048]{1,0:T(8,128)(2,1)S(1)}, bf16[512,2048]{1,0:T(8,128)(2,1)S(1)}, u32[]{:S(2)}, u32[]{:S(2)}) collective-permute-start(bf16[512,2048]{1,0:T(8,128)(2,1)S(1)} %collective-permute-done), channel_id=1, source_target_pairs={{0,4},{4,8},{8,12},{12,16},{16,20},{20,24},{24,28},{28,0},{1,5},{5... | collective-permute-start | bytes 6291464 | tf_op jit(solution)/shard_map/ppermute | solution.py:19
  62.2 1.4 copy-start.7
  63.6 26.4 %collective-permute-start.2 = (bf16[512,2048]{1,0:T(8,128)(2,1)S(1)}, bf16[512,2048]{1,0:T(8,128)(2,1)S(1)}, u32[]{:S(2)}, u32[]{:S(2)}) collective-permute-start(bf16[512,2048]{1,0:T(8,128)(2,1)S(1)} %collective-permute-done.1), channel_id=1, source_target_pairs={{0,4},{4,8},{8,12},{12,16},{16,20},{20,24},{24,28},{28,0},{1,5},{5... | collective-permute-start | bytes 6291464 | tf_op jit(solution)/shard_map/ppermute | solution.py:19
  89.9 1.4 copy-start.9
  91.3 26.4 %collective-permute-start.3 = (bf16[512,2048]{1,0:T(8,128)(2,1)S(1)}, bf16[512,2048]{1,0:T(8,128)(2,1)S(1)}, u32[]{:S(2)}, u32[]{:S(2)}) collective-permute-start(bf16[512,2048]{1,0:T(8,128)(2,1)S(1)} %collective-permute-done.2), channel_id=1, source_target_pairs={{0,4},{4,8},{8,12},{12,16},{16,20},{20,24},{24,28},{28,0},{1,5},{5... | collective-permute-start | bytes 6291464 | tf_op jit(solution)/shard_map/ppermute | solution.py:19
  117.7 1.3 copy-start.11
  119.0 26.4 %collective-permute-start.4 = (bf16[512,2048]{1,0:T(8,128)(2,1)S(1)}, bf16[512,2048]{1,0:T(8,128)(2,1)S(1)}, u32[]{:S(2)}, u32[]{:S(2)}) collective-permute-start(bf16[512,2048]{1,0:T(8,128)(2,1)S(1)} %collective-permute-done.3), channel_id=1, source_target_pairs={{0,4},{4,8},{8,12},{12,16},{16,20},{20,24},{24,28},{28,0},{1,5},{5... | collective-permute-start | bytes 6291464 | tf_op jit(solution)/shard_map/ppermute | solution.py:19
  145.3 1.3 copy-start.13
  146.7 26.5 %collective-permute-start.5 = (bf16[512,2048]{1,0:T(8,128)(2,1)S(1)}, bf16[512,2048]{1,0:T(8,128)(2,1)}, u32[]{:S(2)}, u32[]{:S(2)}) collective-permute-start(bf16[512,2048]{1,0:T(8,128)(2,1)S(1)} %collective-permute-done.4), channel_id=1, source_target_pairs={{0,4},{4,8},{8,12},{12,16},{16,20},{20,24},{24,28},{28,0},{1,5},{5... | collective-permute-start | bytes 6291464 | tf_op jit(solution)/shard_map/ppermute | solution.py:19
  173.2 26.7 %collective-permute-start.6 = (bf16[512,2048]{1,0:T(8,128)(2,1)}, bf16[512,2048]{1,0:T(8,128)(2,1)}, u32[]{:S(2)}, u32[]{:S(2)}) collective-permute-start(bf16[512,2048]{1,0:T(8,128)(2,1)} %collective-permute-done.5), channel_id=1, source_target_pairs={{0,4},{4,8},{8,12},{12,16},{16,20},{20,24},{24,28},{28,0},{1,5},{5... | collective-permute-start | bytes 6291464 | tf_op jit(solution)/shard_map/ppermute | solution.py:19
  177.5 65.9 %copy-start.15 = (bf16[256,32,128]{2,1,0:T(8,128)(2,1)}, bf16[256,32,128]{2,1,0:T(8,128)(2,1)S(1)}, u32[]{:S(2)}) copy-start(bf16[256,32,128]{2,1,0:T(8,128)(2,1)S(1)} %convert_bitcast_fusion) | copy-start | bytes 6291460
  203.0 3.3 copy-start.14
  206.4 2.3 copy-start.12
  208.7 2.3 copy-start.10
  211.1 2.3 copy-start.8
  213.4 2.3 copy-start.6
  215.7 2.3 copy-start.4
  234.8 8.5 %copy-start.19 = (f32[256,32]{0,1:T(8,128)S(1)}, f32[256,32]{0,1:T(8,128)}, u32[]{:S(2)}) copy-start(f32[256,32]{0,1:T(8,128)} %copy.71) | copy-start | bytes 98308
  243.4 12.7 %copy-start.18 = (bf16[256,8,128]{2,1,0:T(8,128)(2,1)S(1)}, bf16[256,8,128]{2,1,0:T(8,128)(2,1)}, u32[]{:S(2)}) copy-start(bf16[256,8,128]{2,1,0:T(8,128)(2,1)} %param.15) | copy-start | bytes 1572868
  246.1 121.9 %all-gather.7.cloned.1.call-start = ((), (), s32[]{:S(2)}) async-start(), calls=%async_computation.2 | async-start | bytes 9437184 | tf_op jit(solution)/shard_map/all_gather | solution.py:50
  256.1 1.6 copy-start.16
  257.7 6.0 %copy-start.2 = (bf16[256,32,128]{2,1,0:T(8,128)(2,1)}, bf16[256,32,128]{2,1,0:T(8,128)(2,1)S(1)}, u32[]{:S(2)}) copy-start(bf16[256,32,128]{2,1,0:T(8,128)(2,1)S(1)} %convert_bitcast_fusion.1) | copy-start | bytes 6291460
  263.7 2.0 copy-start.3
  284.1 10.7 %copy-start.21 = (f32[32]{0:T(128)S(1)}, f32[32]{0:T(128)}, u32[]{:S(2)}) copy-start(f32[32]{0:T(128)} %param.18) | copy-start | bytes 388
  301.1 2.0 copy-start.17
  313.4 135.4 %reduce-scatter.2.cloned.1.call-start = ((), (), s32[]{:S(2)}) async-start(), calls=%async_computation.1 | async-start | bytes 2621440 | tf_op jit(solution)/shard_map/reduce_scatter | solution.py:169
  376.3 10.5 %copy-start.20 = (f32[256,32]{0,1:T(8,128)S(1)}, f32[256,32]{0,1:T(8,128)}, u32[]{:S(2)}) copy-start(f32[256,32]{0,1:T(8,128)} %copy.71) | copy-start | bytes 98308
  392.7 56.1 %copy-start.1 = (bf16[256,4096]{1,0:T(8,128)(2,1)S(1)}, bf16[256,4096]{1,0:T(8,128)(2,1)}, u32[]{:S(2)}) copy-start(bf16[256,4096]{1,0:T(8,128)(2,1)} %param.12) | copy-start | bytes 6291460
Sparse Core Ops, SparseCore 0:
  246.2 37.7 all-gather.8
  313.6 54.3 all-gather.6
  404.9 43.8 reduce-scatter.1
